TPU v7x, 32 devices: a whole 2x2x4 slice. The times are simulated.
32 devices in a mesh: sect: 4 (over y, x), dev: 8 (over z, core).
Axes of the slice: x: 2, y: 2, z: 4, core: 2. Of those that a mesh axis runs over, the one named last changes fastest.
Arguments:
- voltages: bfloat16 [2, 2048, 65536], P(None, 'sect', 'dev'), may hold values from -6 to 6
- filter_taps: float32 [4, 1024], replicated, may hold values from -3 to 3
- feed_tile: int32 [2048], P('sect'), may hold values from 0 to 127
- bad_feed: int32 [2048], P('sect'), may hold values 0 or 1
- delays: float32 [1024, 128], P('sect'), may hold values from -32 to 32
Outputs:
- visibilities: float32 [2, 1024, 128, 128], P(None, 'dev', 'sect')
- beams: bfloat16 [2, 1024, 1024, 64], P(None, 'dev', 'sect')
Inputs may be any that keep to these rules, and one draw needn't show every extreme that they name: `feed_tile`: each feed belongs to one tile.
All inputs are finite; a program needn't handle non-finite values. No bound on the sum of `bad_feed` on one device may be relied on, other than what follows from the above.
Results may differ from a plain program's by a relative error of at most 0.014.
Values may be sent and summed in bfloat16 or wider, within the bound.
A program may use at most 192 MiB of HBM per device.

v0:
```python
import math

import jax
import jax.numpy as jnp
from jax import lax
from jax.sharding import PartitionSpec as P

FEEDS = 2048
TILES = 128
TAPS = 4


def shifted(x, axis, by):
    size = lax.axis_size(axis)
    pairs = [(i, i + by) for i in range(size) if 0 <= i + by < size]
    return lax.ppermute(x, axis, pairs)


def turn_trig(turns):
    r = turns - jnp.round(turns)
    y = r * math.pi
    q = y * y
    s = 0.0
    for n in (11, 9, 7, 5, 3, 1):
        s = s * q + (-1.0) ** ((n - 1) // 2) / math.factorial(n)
    s = s * y
    c = 0.0
    for n in (12, 10, 8, 6, 4, 2, 0):
        c = c * q + (-1.0) ** (n // 2) / math.factorial(n)
    return 1.0 - 2.0 * s * s, 2.0 * s * c


def fourier_tables(channels):
    low = 32
    c = jnp.arange(channels, dtype=jnp.int32)[None, :]
    k_high = low * jnp.arange(channels // low, dtype=jnp.int32)[:, None]
    k_low = jnp.arange(low, dtype=jnp.int32)[:, None]
    ca, sa = turn_trig((k_high * c % channels).astype(jnp.float32) / channels)
    cb, sb = turn_trig((k_low * c % channels).astype(jnp.float32) / channels)
    factor = 1.0 / math.sqrt(channels)
    ca, sa = (ca * factor)[:, None], (sa * factor)[:, None]
    cb, sb = cb[None], sb[None]
    cosine = (ca * cb - sa * sb).astype(jnp.bfloat16).reshape(channels, channels)
    sine = (sa * cb + ca * sb).astype(jnp.bfloat16).reshape(channels, channels)
    return cosine, sine


def beam_weights(delays, first, count, channels):
    low = 16
    d = delays.T[None]
    high = (first + low * jnp.arange(count // low, dtype=jnp.int32)).astype(jnp.float32)
    ca, sa = turn_trig(d * high[:, None, None] / channels)
    cb, sb = turn_trig(d * jnp.arange(low, dtype=jnp.float32)[:, None, None] / channels)
    ca, sa, cb, sb = ca[:, None], sa[:, None], cb[None], sb[None]
    shape = (count,) + d.shape[1:]
    cosine = (ca * cb - sa * sb).astype(jnp.bfloat16).reshape(shape)
    sine = (sa * cb + ca * sb).astype(jnp.bfloat16).reshape(shape)
    return jnp.concatenate([cosine, sine], axis=1)


def local(voltages, filter_taps, feed_tile, bad_feed, delays):
    channels = filter_taps.shape[1]
    local_frames = voltages.shape[2] // channels
    rim = (TAPS - 1) * channels
    n_dev = lax.axis_size("dev")
    local_chans = channels // n_dev
    total_frames = local_frames * n_dev

    tile_ids = jnp.arange(TILES, dtype=jnp.int32)
    member = (feed_tile[None, :] == tile_ids[:, None]) & (bad_feed[None, :] == 0)
    matrix = jnp.where(member, 1.0, 0.0).astype(jnp.bfloat16)
    partial_value = jnp.einsum(
        "af,zfs->zas", matrix, voltages, preferred_element_type=jnp.float32
    ).astype(jnp.bfloat16)
    summed = lax.psum_scatter(partial_value, "sect", scatter_dimension=1, tiled=True)
    own = summed.shape[1]

    history = shifted(summed[:, :, summed.shape[2] - rim :], "dev", 1)
    window = jnp.concatenate([history, summed], axis=2).reshape(
        2, own, local_frames + TAPS - 1, channels
    )
    running = 0.0
    for tap in range(TAPS):
        begin = TAPS - 1 - tap
        running = running + filter_taps[tap] * window[:, :, begin : begin + local_frames].astype(
            jnp.float32
        )
    filtered = running.astype(jnp.bfloat16)

    cosine, sine = fourier_tables(channels)
    dot = lambda a, b: jnp.dot(a, b, preferred_element_type=jnp.float32)
    spectra = jnp.stack(
        [
            dot(filtered[0], cosine) + dot(filtered[1], sine),
            dot(filtered[1], cosine) - dot(filtered[0], sine),
        ]
    ).astype(jnp.bfloat16)

    own_tiles = lax.all_to_all(spectra, "dev", split_axis=3, concat_axis=2, tiled=True)
    gathered = lax.all_gather(own_tiles, "sect", axis=1, tiled=True)

    volts = jnp.transpose(gathered, (3, 0, 2, 1))
    mine = jnp.transpose(own_tiles, (3, 0, 1, 2))
    left_real = jnp.concatenate([mine[:, 0], mine[:, 1]], axis=2)
    left_quad = jnp.concatenate([mine[:, 1], -mine[:, 0]], axis=2)
    left = jnp.concatenate([left_real, left_quad], axis=1)
    right = volts.reshape(local_chans, 2 * total_frames, TILES)
    vis = jnp.einsum("cat,ctb->cab", left, right, preferred_element_type=jnp.float32)
    vis_scale = 1.0 / (total_frames * FEEDS / TILES)
    vis = vis * vis_scale
    visibility = jnp.stack([vis[:, :own], vis[:, own:]])

    weights = beam_weights(
        delays, lax.axis_index("dev") * local_chans, local_chans, channels
    )
    rows = jnp.concatenate(
        [
            jnp.concatenate([volts[:, 0], volts[:, 1]], axis=2),
            jnp.concatenate([volts[:, 1], -volts[:, 0]], axis=2),
        ],
        axis=1,
    )
    beams = jnp.einsum("cna,cab->cnb", rows, weights, preferred_element_type=jnp.float32)
    beams = (beams * (1.0 / math.sqrt(FEEDS))).astype(jnp.bfloat16)
    beams = beams.reshape(local_chans, 2, total_frames, weights.shape[2])
    return visibility, jnp.transpose(beams, (1, 0, 3, 2))


def solution(mesh):
    return jax.shard_map(
        local,
        mesh=mesh,
        in_specs=(P(None, "sect", "dev"), P(), P("sect"), P("sect"), P("sect", None)),
        out_specs=(P(None, "dev", "sect", None), P(None, "dev", "sect", None)),
        check_vma=False,
    )
```

profile of v0, /device:TPU:0, one launch (start us, length us, event | category | flops | bytes accessed | tf_op | source)
XLA Modules:
  0.0 255.6 jit_solution(14629672204459343020)
XLA Ops:
  7.9 10.2 %fusion.4 = bf16[2,128,8192]{2,1,0:T(8,128)(2,1)} fusion(bf16[2,512,8192]{2,1,0:T(8,128)(2,1)} %param.5, s32[512]{0:T(512)} %param.7, pred[512]{0:T(512)(128)(4,1)S(1)} %broadcast_compare_fusion), kind=kOutput, calls=%fused_computation.8 | convolution fusion | flops 2149842944 | bytes 20974080 | tf_op jit(solution)/shard_map/af,zfs->zas/dot_general | solution.py:72
  19.2 54.3 %reduce-scatter.2.cloned.1.call-done = bf16[2,32,8192]{2,1,0:T(8,128)(2,1)} async-done(((bf16[2,128,8192]{2,1,0:T(8,128)(2,1)}), bf16[2,32,8192]{2,1,0:T(8,128)(2,1)}) %reduce-scatter.2.cloned.1.call-update) | async-done | bytes 1048592 | tf_op jit(solution)/shard_map/reduce_scatter | solution.py:75
  74.6 1.6 collective-permute-start
  76.3 2.6 %add_convert_fusion.1 = (bf16[32,32,1024]{2,1,0:T(8,128)(2,1)}, bf16[32,32,1024]{2,1,0:T(8,128)(2,1)S(1)}) fusion(f32[32,1024]{1,0:T(8,128)S(1)} %get-tuple-element.22, f32[32,1024]{1,0:T(8,128)S(1)} %get-tuple-element.21, f32[32,1024]{1,0:T(8,128)S(1)} %fusion.45, f32[32,1024]{1,0:T(8,128)S(1)} %get-tuple-element.20), kind=kLoop, calls=%fused_computation.18 | loop fusion | flops 8388608 | bytes 4718592 | tf_op jit(solution)/shard_map/convert_element_type | solution.py:44
  79.0 1.9 reshape.326
  81.0 5.2 %add_convert_fusion.2 = bf16[2,32,8,1024]{3,2,1,0:T(8,128)(2,1)S(1)} fusion(bf16[2,32,11,1024]{3,2,1,0:T(8,128)(2,1)} %reshape.326, f32[1024]{0:T(1024)S(1)} %bitcast.88, f32[1024]{0:T(1024)S(1)} %bitcast.89, f32[1024]{0:T(1024)S(1)} %bitcast.87, f32[1024]{0:T(1024)S(1)} %bitcast.86), kind=kLoop, calls=%fused_computation.46 | loop fusion | flops 6291456 | bytes 5259264 | tf_op jit(solution)/shard_map/convert_element_type | solution.py:88
  90.1 5.0 %copy.37 = bf16[2,32,8,1024]{1,2,0,3:T(8,128)(2,1)} copy(bf16[2,32,8,1024]{3,2,1,0:T(8,128)(2,1)S(1)} %pad_maximum_fusion.2) | data formatting | bytes 2097152 | tf_op jit(solution)/shard_map/stack | solution.py:92
  95.1 7.0 %reshape.332 = bf16[8,2,32768]{2,1,0:T(2,128)(2,1)S(1)} reshape(bf16[1024,2,8,32]{3,2,1,0:T(8,128)(2,1)} %bitcast.73) | data formatting | bytes 2097152
  102.1 35.7 %all_to_all.18 = bf16[8,2,32768]{2,1,0:T(2,128)(2,1)S(1)} all-to-all(bf16[8,2,32768]{2,1,0:T(2,128)(2,1)S(1)} %reshape.332), channel_id=1, replica_groups=mesh['sect'=4,'dev'=8] {'dev'}, dimensions={0} | all-to-all | bytes 2097152 | tf_op jit(solution)/shard_map/all_to_all | solution.py:99
  137.7 4.5 %reshape.333 = bf16[1024,2,8,32]{3,2,1,0:T(8,128)(2,1)} reshape(bf16[8,2,32768]{2,1,0:T(2,128)(2,1)S(1)} %all_to_all.18) | data formatting | bytes 2097152
  142.2 5.0 %copy.39 = bf16[2,32,8,8,128]{4,3,2,1,0:T(8,128)(2,1)S(1)} copy(bf16[2,32,8,8,128]{1,3,0,4,2:T(8,128)(2,1)} %bitcast.74) | data formatting | bytes 2097152 | tf_op jit(solution)/shard_map/all_to_all | solution.py:99
  149.7 2.5 fusion.16
  152.2 8.1 %subtract_convert_fusion = (bf16[8,16,128,256]{3,2,1,0:T(8,128)(2,1)}, bf16[8,16,128,256]{3,2,1,0:T(8,128)(2,1)}) fusion(f32[16,128,256]{2,1,0:T(8,128)S(1)} %get-tuple-element.15, f32[8,128,256]{2,1,0:T(8,128)S(1)} %get-tuple-element.13, f32[16,128,256]{2,1,0:T(8,128)S(1)} %get-tuple-element.14, f32[8,128,256]{2,1,0:T(8,128)S(1)} %get-tuple-element.12), kind=kLoop, calls=%fused_computation.6 | loop fusion | flops 33554432 | bytes 23068672 | tf_op jit(solution)/shard_map/convert_element_type | solution.py:56
  160.3 2.9 %copy.40 = bf16[2,32,64,128]{2,1,3,0:T(8,128)(2,1)S(1)} copy(bf16[2,32,64,128]{3,2,1,0:T(8,128)(2,1)S(1)} %bitcast.80) | data formatting | bytes 2097152 | tf_op jit(solution)/shard_map/all_to_all | solution.py:99
  163.4 1.7 slice_bitcast_fusion.5
  165.0 34.0 %all-gather.2.cloned.1.call-done = bf16[2,128,64,128]{3,2,0,1:T(8,128)(2,1)} async-done(((bf16[2,32,64,128]{3,2,0,1:T(8,128)(2,1)}), bf16[2,128,64,128]{3,2,0,1:T(8,128)(2,1)}) %all-gather.2.cloned.1.call-update) | async-done | bytes 4194320 | tf_op jit(solution)/shard_map/all_gather | solution.py:100
  199.0 7.3 %copy.42 = bf16[2,128,64,128]{1,2,3,0:T(8,128)(2,1)} copy(bf16[2,128,64,128]{3,2,0,1:T(8,128)(2,1)} %all-gather.2.cloned.1.call-done) | data formatting | bytes 8388608 | tf_op jit(solution)/shard_map/all_gather | solution.py:100
  206.3 3.3 %fusion.79 = bf16[128,64,128]{2,1,0:T(8,128)(2,1)} fusion(bf16[128,2,64,128]{3,2,0,1:T(8,128)(2,1)} %bitcast.67), kind=kLoop, calls=%fused_computation.139 | loop fusion | flops 1048576 | bytes 4194304 | tf_op jit(solution)/shard_map/neg | solution.py:119
  209.6 2.9 %slice_bitcast_fusion.1 = (bf16[128,64,128]{2,1,0:T(8,128)(2,1)}, bf16[128,64,128]{2,1,0:T(8,128)(2,1)}) fusion(bf16[128,2,64,128]{3,2,0,1:T(8,128)(2,1)S(1)} %bitcast.68), kind=kLoop, calls=%fused_computation.27 | loop fusion | bytes 8388608 | tf_op jit(solution)/shard_map/squeeze | solution.py:118
  212.6 7.5 %copy.43 = bf16[128,2,64,128]{3,2,1,0:T(8,128)(2,1)} copy(bf16[128,2,64,128]{0,2,1,3:T(8,128)(2,1)} %bitcast.75) | data formatting | bytes 8388608 | tf_op jit(solution)/shard_map/transpose | solution.py:102
  220.0 3.6 %convolution_multiply_fusion = f32[128,64,128]{2,1,0:T(8,128)S(1)} fusion(bf16[128,128,128]{2,1,0:T(8,128)(2,1)} %bitcast.76, bf16[128,32,64]{2,1,0:T(8,128)(2,1)S(1)} %fusion.78, bf16[128,32,64]{2,1,0:T(8,128)(2,1)S(1)} %copy-done.3, bf16[128,32,64]{2,1,0:T(8,128)(2,1)S(1)} %copy-done.2), kind=kOutput, calls=%fused_computation.23 | convolution fusion | flops 277872640 | bytes 9961472 | tf_op jit(solution)/shard_map/cat,ctb->cab/dot_general | solution.py:108
  226.5 11.4 %multiply_convert_fusion = bf16[128,128,256]{2,1,0:T(8,128)(2,1)} fusion(bf16[128,128,256]{2,1,0:T(8,128)(2,1)} %bitcast.84, bf16[128,128,256]{2,1,0:T(8,128)(2,1)} %bitcast.83, bf16[128,64,128]{2,1,0:T(8,128)(2,1)S(1)} %copy-done.4, bf16[128,64,128]{2,1,0:T(8,128)(2,1)S(1)} %copy-done.6, bf16[128,64,128]{2,1,0:T(8,128)(2,1)S(1)} %copy-done.5), kind=kOutput, calls=%fused_computation.4 | convolution fusion | flops 2222981120 | bytes 31457280 | tf_op jit(solution)/shard_map/cna,cab->cnb/dot_general | solution.py:123
  237.9 8.4 %copy.51 = bf16[128,2,64,256]{3,2,0,1:T(8,128)(2,1)} copy(bf16[128,2,64,256]{3,2,1,0:T(8,128)(2,1)} %bitcast.82) | data formatting | bytes 16777216 | tf_op jit(solution)/shard_map/reshape | solution.py:125
  246.3 2.5 pad_maximum_fusion
  (43 shorter events, 12.5 us)
Async XLA Ops:
  7.2 66.4 %reduce-scatter.2.cloned.1.call-start = ((), (), s32[]{:S(2)}) async-start(), calls=%async_computation.2 | async-start | bytes 5242880 | tf_op jit(solution)/shard_map/reduce_scatter | solution.py:75
  18.1 0.7 copy-start.9
  18.1 180.9 %all-gather.2.cloned.1.call-start = ((), (), s32[]{:S(2)}) async-start(), calls=%async_computation.3 | async-start | bytes 5242880 | tf_op jit(solution)/shard_map/all_gather | solution.py:100
  74.6 4.4 %collective-permute-start = (bf16[2,32,3072]{2,1,0:T(8,128)(2,1)S(1)}, bf16[2,32,3072]{2,1,0:T(8,128)(2,1)S(1)}, u32[]{:S(2)}, u32[]{:S(2)}) collective-permute-start(bf16[2,32,3072]{2,1,0:T(8,128)(2,1)S(1)} %slice.74), channel_id=1, source_target_pairs={{0,1},{1,2},{2,3},{3,4},{4,5},{5,6},{6,7},{8,9},{9,10},{10,11},{11... | collective-permute-start | bytes 1179656 | tf_op jit(solution)/shard_map/ppermute | solution.py:16
  76.3 2.6 %copy-start.7 = (bf16[2,32,8192]{2,1,0:T(8,128)(2,1)S(1)}, bf16[2,32,8192]{2,1,0:T(8,128)(2,1)}, u32[]{:S(2)}) copy-start(bf16[2,32,8192]{2,1,0:T(8,128)(2,1)} %reduce-scatter.2.cloned.1.call-done) | copy-start | bytes 3145732
  86.9 1.6 copy-start.1
  147.2 1.1 copy-start.8
  206.3 3.3 %copy-start = (bf16[2,128,64,128]{1,2,3,0:T(8,128)(2,1)S(1)}, bf16[2,128,64,128]{1,2,3,0:T(8,128)(2,1)}, u32[]{:S(2)}) copy-start(bf16[2,128,64,128]{1,2,3,0:T(8,128)(2,1)} %copy.42) | copy-start | bytes 12582916
  212.6 7.5 %copy-start.2 = (bf16[128,32,64]{2,1,0:T(8,128)(2,1)S(1)}, bf16[128,32,64]{2,1,0:T(8,128)(2,1)}, u32[]{:S(2)}) copy-start(bf16[128,32,64]{2,1,0:T(8,128)(2,1)} %get-tuple-element.8) | copy-start | bytes 1572868
  212.6 7.5 %copy-start.3 = (bf16[128,32,64]{2,1,0:T(8,128)(2,1)S(1)}, bf16[128,32,64]{2,1,0:T(8,128)(2,1)}, u32[]{:S(2)}) copy-start(bf16[128,32,64]{2,1,0:T(8,128)(2,1)} %get-tuple-element.9) | copy-start | bytes 1572868
  223.6 1.6 copy-start.4
  223.6 2.2 copy-start.5
  223.6 2.8 %copy-start.6 = (bf16[128,64,128]{2,1,0:T(8,128)(2,1)S(1)}, bf16[128,64,128]{2,1,0:T(8,128)(2,1)}, u32[]{:S(2)}) copy-start(bf16[128,64,128]{2,1,0:T(8,128)(2,1)} %get-tuple-element.5) | copy-start | bytes 6291460
Sparse Core Ops, SparseCore 0:
  18.2 55.3 reduce-scatter.1
  148.4 50.5 all-gather.1
where the time goes:
time: 256 us
  waiting for transfers between devices  88.3 us (34%)
  local copies, waits for them, and re-layouts  60.7 us (24%)
  blocking collectives  35.7 us (14%)
  matrix products  28 us (11%)
  other arithmetic  27 us (11%)
  between operations  14.3 us (6%)
    reduce_scatter x1, waiting for transfers between devices, local(): lax.psum_scatter(partial_value, 'sect', scatter_dimension=1, tiled=True)  54.3 us
    all_to_all x1, blocking collectives, local(): lax.all_to_all(spectra, 'dev', split_axis=3, concat_axis=2, tiled=True)  35.7 us
    all_gather x1, waiting for transfers between devices, local(): gathered = lax.all_gather(own_tiles, 'sect', axis=1, tiled=True)  34 us
    unnamed x22, local copies, waits for them, and re-layouts  15.2 us
    dot_general x1, matrix products, local(): jnp.einsum('cna,cab->cnb', rows, weights, preferred_element_type=jnp.floa...  11.4 us
    dot_general x1, matrix products, local(): jnp.einsum('af,zfs->zas', matrix, voltages, preferred_element_type=jnp.fl...  10.2 us
    all_to_all x3, local copies, waits for them, and re-layouts, local(): lax.all_to_all(spectra, 'dev', split_axis=3, concat_axis=2, tiled=True)  9.02 us
    reshape x1, local copies, waits for them, and re-layouts, local(): beams = beams.reshape(local_chans, 2, total_frames, weights.shape[2])  8.44 us
  transfers between devices with their start and end apart: 3, of which 2 were waited for; matrix products, arithmetic and copies ran while one was open for 8% of the time, Pallas kernels for 0%

commit v1 on v0

--- a/solution.py
+++ b/solution.py
@@ -1,8 +1,11 @@
+import functools
 import math
 
 import jax
 import jax.numpy as jnp
 from jax import lax
+from jax.experimental import pallas as pl
+from jax.experimental.pallas import tpu as pltpu
 from jax.sharding import PartitionSpec as P
 
 FEEDS = 2048
@@ -58,11 +61,180 @@
     return jnp.concatenate([cosine, sine], axis=1)
 
 
+VMEM = pl.BlockSpec(memory_space=pltpu.VMEM)
+
+
+def transform_kernel(summed, history, taps, cosine, sine, out, filtered):
+    n_dest, _, _, width = out.shape
+    own = summed.shape[1]
+    channels = taps.shape[1]
+    frames = summed.shape[2] // channels
+    for z in range(2):
+        for t in range(frames):
+            total = 0.0
+            for m in range(TAPS):
+                if t >= m:
+                    block = summed[z, :, (t - m) * channels : (t - m + 1) * channels]
+                else:
+                    at = t - m + TAPS - 1
+                    block = history[z, :, at * channels : (at + 1) * channels]
+                total = total + taps[m : m + 1, :] * block.astype(jnp.float32)
+            filtered[z, t * own : (t + 1) * own, :] = total.astype(jnp.bfloat16)
+    step = max(256, width)
+    dot = lambda a, b: jnp.dot(a, b, preferred_element_type=jnp.float32)
+    for begin in range(0, channels, step):
+        c, s = cosine[:, begin : begin + step], sine[:, begin : begin + step]
+        real = (dot(filtered[0], c) + dot(filtered[1], s)).astype(jnp.bfloat16)
+        quad = (dot(filtered[1], c) - dot(filtered[0], s)).astype(jnp.bfloat16)
+        for j in range(step // width):
+            out[begin // width + j, 0] = real[:, j * width : (j + 1) * width]
+            out[begin // width + j, 1] = quad[:, j * width : (j + 1) * width]
+
+
+def exchange_kernel(n_sect, n_dev, src, out, own_sem, a_send, a_recv, x_send, x_recv, y_send, y_recv):
+    me_s, me_d = lax.axis_index("sect"), lax.axis_index("dev")
+    rows = n_sect // 2
+    side, row = lax.rem(me_s, 2), me_s // 2
+    across = row * 2 + 1 - side
+    others = [(lax.rem(row + j, rows) * 2 + side) for j in range(1, rows)]
+    senders = [(lax.rem(row + rows - j, rows) * 2 + side) for j in range(1, rows)]
+
+    barrier = pltpu.get_barrier_semaphore()
+    mesh_id = pl.DeviceIdType.MESH
+    for o in range(1, n_dev):
+        pl.semaphore_signal(barrier, inc=1, device_id=(me_s, lax.rem(me_d + o, n_dev)), device_id_type=mesh_id)
+    for s in [across] + others:
+        pl.semaphore_signal(barrier, inc=1, device_id=(s, me_d), device_id_type=mesh_id)
+    pl.semaphore_wait(barrier, n_dev - 1 + rows)
+
+    def push(source, target, send, recv, device):
+        return pltpu.make_async_remote_copy(
+            src_ref=source, dst_ref=target, send_sem=send, recv_sem=recv,
+            device_id=device, device_id_type=mesh_id,
+        )
+
+    order = [0] + [o for pair in zip(range(1, n_dev), range(n_dev - 1, 0, -1)) for o in pair][: n_dev - 1]
+    keep = pltpu.make_async_copy(src.at[me_d], out.at[me_s, me_d], own_sem)
+    keep.start()
+    sends = []
+    to_dev = {}
+    for o in order[1:]:
+        dest = lax.rem(me_d + o, n_dev)
+        to_dev[o] = push(src.at[dest], out.at[me_s, me_d], a_send.at[o], a_recv.at[o], (me_s, dest))
+        to_dev[o].start()
+    keep.wait()
+
+    first = {}
+
+    def spread(o):
+        p = lax.rem(me_d + n_dev - o, n_dev)
+        here = out.at[me_s, p]
+        if o:
+            to_dev[o].wait_recv()
+        first[o, 0] = push(here, here, x_send.at[o, 0], x_recv.at[o, 0], (across, me_d))
+        first[o, 0].start()
+        for j in range(1, rows):
+            first[o, j] = push(here, here, y_send.at[o, j, 0], y_recv.at[o, j, 0], (others[j - 1], me_d))
+            first[o, j].start()
+
+    def relay(o, by_side):
+        p = lax.rem(me_d + n_dev - o, n_dev)
+        first[o, 0].wait_recv()
+        for j in range(1, rows):
+            first[o, j].wait_recv()
+        for j in range(1, rows):
+            if by_side:
+                block = out.at[across, p]
+                copy = push(block, block, y_send.at[o, j, 1], y_recv.at[o, j, 1], (others[j - 1], me_d))
+            else:
+                block = out.at[senders[j - 1], p]
+                copy = push(block, block, x_send.at[o, j], x_recv.at[o, j], (across, me_d))
+            copy.start()
+            sends.append(copy)
+
+    lag = 1
+    for i in range(n_dev + lag):
+        if i < n_dev:
+            spread(order[i])
+        if i >= lag:
+            relay(order[i - lag], (i - lag) % 2 == 0)
+    for copy in sends:
+        copy.wait_recv()
+    for copy in list(to_dev.values()) + list(first.values()) + sends:
+        copy.wait_send()
+
+
+def exchange(blocks, n_sect, n_dev):
+    rows = n_sect // 2
+    dma = pltpu.SemaphoreType.DMA
+    return pl.pallas_call(
+        functools.partial(exchange_kernel, n_sect, n_dev),
+        out_shape=jax.ShapeDtypeStruct((n_sect,) + blocks.shape, blocks.dtype),
+        in_specs=[VMEM],
+        out_specs=VMEM,
+        scratch_shapes=[
+            dma, dma((n_dev,)), dma((n_dev,)),
+            dma((n_dev, rows)), dma((n_dev, rows)),
+            dma((n_dev, rows, 2)), dma((n_dev, rows, 2)),
+        ],
+        compiler_params=pltpu.CompilerParams(
+            collective_id=0, has_side_effects=True, vmem_limit_bytes=32 * 2**20
+        ),
+    )(blocks)
+
+
+def product_kernel(own, vis_scale, beam_scale, volts, weights, vis, beams, full):
+    first = pl.multiple_of(lax.axis_index("sect") * own, own)
+    count, both, _ = volts.shape
+    half = both // 2
+
+    @pl.loop(0, count)
+    def _(c):
+        real, quad = volts[c, :half, :], volts[c, half:, :]
+        rows = jnp.concatenate(
+            [jnp.concatenate([real, quad], axis=1), jnp.concatenate([quad, -real], axis=1)], axis=0
+        )
+        beam = jnp.dot(rows, weights[c], preferred_element_type=jnp.float32) * beam_scale
+        beams[0, c] = beam[:half].astype(jnp.bfloat16)
+        beams[1, c] = beam[half:].astype(jnp.bfloat16)
+        right = jnp.concatenate([real, quad], axis=0)
+        turned = jnp.concatenate([quad, -real], axis=0)
+        over_time = (((0,), (0,)), ((), ()))
+        full[0] = lax.dot_general(right, right, over_time, preferred_element_type=jnp.float32)
+        full[1] = lax.dot_general(turned, right, over_time, preferred_element_type=jnp.float32)
+        vis[0, c] = full[0, pl.ds(first, own), :] * vis_scale
+        vis[1, c] = full[1, pl.ds(first, own), :] * vis_scale
+
+
+def products(volts, weights, own, vis_scale, beam_scale):
+    chans, both, tiles = volts.shape
+    beams = weights.shape[2]
+    block = 8
+    return pl.pallas_call(
+        functools.partial(product_kernel, own, vis_scale, beam_scale),
+        grid=(chans // block,),
+        out_shape=(
+            jax.ShapeDtypeStruct((2, chans, own, tiles), jnp.float32),
+            jax.ShapeDtypeStruct((2, chans, both // 2, beams), jnp.bfloat16),
+        ),
+        in_specs=[
+            pl.BlockSpec((block, both, tiles), lambda i: (i, 0, 0)),
+            pl.BlockSpec((block, 2 * tiles, beams), lambda i: (i, 0, 0)),
+        ],
+        out_specs=(
+            pl.BlockSpec((2, block, own, tiles), lambda i: (0, i, 0, 0)),
+            pl.BlockSpec((2, block, both // 2, beams), lambda i: (0, i, 0, 0)),
+        ),
+        scratch_shapes=[pltpu.VMEM((2, tiles, tiles), jnp.float32)],
+    )(volts, weights)
+
+
 def local(voltages, filter_taps, feed_tile, bad_feed, delays):
     channels = filter_taps.shape[1]
     local_frames = voltages.shape[2] // channels
     rim = (TAPS - 1) * channels
     n_dev = lax.axis_size("dev")
+    n_sect = lax.axis_size("sect")
     local_chans = channels // n_dev
     total_frames = local_frames * n_dev
 
@@ -75,55 +247,30 @@
     summed = lax.psum_scatter(partial_value, "sect", scatter_dimension=1, tiled=True)
     own = summed.shape[1]
 
-    history = shifted(summed[:, :, summed.shape[2] - rim :], "dev", 1)
-    window = jnp.concatenate([history, summed], axis=2).reshape(
-        2, own, local_frames + TAPS - 1, channels
-    )
-    running = 0.0
-    for tap in range(TAPS):
-        begin = TAPS - 1 - tap
-        running = running + filter_taps[tap] * window[:, :, begin : begin + local_frames].astype(
-            jnp.float32
-        )
-    filtered = running.astype(jnp.bfloat16)
-
     cosine, sine = fourier_tables(channels)
-    dot = lambda a, b: jnp.dot(a, b, preferred_element_type=jnp.float32)
-    spectra = jnp.stack(
-        [
-            dot(filtered[0], cosine) + dot(filtered[1], sine),
-            dot(filtered[1], cosine) - dot(filtered[0], sine),
-        ]
-    ).astype(jnp.bfloat16)
-
-    own_tiles = lax.all_to_all(spectra, "dev", split_axis=3, concat_axis=2, tiled=True)
-    gathered = lax.all_gather(own_tiles, "sect", axis=1, tiled=True)
-
-    volts = jnp.transpose(gathered, (3, 0, 2, 1))
-    mine = jnp.transpose(own_tiles, (3, 0, 1, 2))
-    left_real = jnp.concatenate([mine[:, 0], mine[:, 1]], axis=2)
-    left_quad = jnp.concatenate([mine[:, 1], -mine[:, 0]], axis=2)
-    left = jnp.concatenate([left_real, left_quad], axis=1)
-    right = volts.reshape(local_chans, 2 * total_frames, TILES)
-    vis = jnp.einsum("cat,ctb->cab", left, right, preferred_element_type=jnp.float32)
-    vis_scale = 1.0 / (total_frames * FEEDS / TILES)
-    vis = vis * vis_scale
-    visibility = jnp.stack([vis[:, :own], vis[:, own:]])
-
     weights = beam_weights(
         delays, lax.axis_index("dev") * local_chans, local_chans, channels
     )
-    rows = jnp.concatenate(
-        [
-            jnp.concatenate([volts[:, 0], volts[:, 1]], axis=2),
-            jnp.concatenate([volts[:, 1], -volts[:, 0]], axis=2),
-        ],
-        axis=1,
-    )
-    beams = jnp.einsum("cna,cab->cnb", rows, weights, preferred_element_type=jnp.float32)
-    beams = (beams * (1.0 / math.sqrt(FEEDS))).astype(jnp.bfloat16)
-    beams = beams.reshape(local_chans, 2, total_frames, weights.shape[2])
-    return visibility, jnp.transpose(beams, (1, 0, 3, 2))
+    summed, cosine, sine, weights = lax.optimization_barrier((summed, cosine, sine, weights))
+
+    history = shifted(summed[:, :, summed.shape[2] - rim :], "dev", 1)
+    blocks = pl.pallas_call(
+        transform_kernel,
+        out_shape=jax.ShapeDtypeStruct((n_dev, 2, local_frames * own, local_chans), jnp.bfloat16),
+        in_specs=[VMEM] * 5,
+        out_specs=VMEM,
+        scratch_shapes=[pltpu.VMEM((2, local_frames * own, channels), jnp.bfloat16)],
+    )(summed, history, filter_taps, cosine, sine)
+    blocks = blocks.reshape(n_dev, 2 * local_frames * own, local_chans)
+    gathered = exchange(blocks, n_sect, n_dev)
+    gathered = gathered.reshape(n_sect, n_dev, 2, local_frames, own, local_chans)
+    volts = jnp.transpose(gathered, (5, 2, 1, 3, 0, 4)).reshape(
+        local_chans, 2 * total_frames, TILES
+    )
+    vis, beams = products(
+        volts, weights, own, 1.0 / (total_frames * FEEDS / TILES), 1.0 / math.sqrt(FEEDS)
+    )
+    return vis, jnp.transpose(beams, (0, 1, 3, 2))
 
 
 def solution(mesh):

time: 256 us -> 183 us (0.71)
  Pallas kernels: 0 us -> 85.9 us
  waiting for transfers between devices: 88.3 us -> 36.6 us
  local copies, waits for them, and re-layouts: 60.7 us -> 14 us
  blocking collectives: 35.7 us -> 0 us
  matrix products: 28 us -> 10.2 us
  other arithmetic: 27 us -> 19.7 us
    pallas_call x0 -> x3, Pallas kernels: none -> 85.9 us  [the longest x1 50 us: exchange(): pl.pallas_call(functools.partial(exchange_kernel, n_sect, n_dev), out_sha...]
    all_to_all x1 -> x0, blocking collectives: 35.7 us -> none  [local(): lax.all_to_all(spectra, 'dev', split_axis=3, concat_axis=2, tiled=True)]
    all_gather x1 -> x0, waiting for transfers between devices: 34 us -> none  [local(): gathered = lax.all_gather(own_tiles, 'sect', axis=1, tiled=True)]
    reduce_scatter x1, waiting for transfers between devices: 54.3 us -> 35.4 us  [local(): lax.psum_scatter(partial_value, 'sect', scatter_dimension=1, tiled=True)]
    dot_general x6 -> x0, matrix products: 17.8 us -> none  [the longest x1 11.4 us: local(): jnp.einsum('cna,cab->cnb', rows, weights, preferred_element_type=jnp.floa...]
    unnamed x22 -> x6, local copies, waits for them, and re-layouts: 15.2 us -> 2.85 us
    all_to_all x3 -> x0, local copies, waits for them, and re-layouts: 9.02 us -> none  [local(): lax.all_to_all(spectra, 'dev', split_axis=3, concat_axis=2, tiled=True)]
    transpose x1 -> x0, local copies, waits for them, and re-layouts: 7.45 us -> none  [local(): volts = jnp.transpose(gathered, (3, 0, 2, 1))]
  transfers between devices with their start and end apart: 3 -> 2, of which waited for: 2 -> 2; matrix products, arithmetic and copies ran while one was open for 8% -> 10% of each run, Pallas kernels for 0% -> 0%
where the time goes in v1:
time: 183 us; the launch traced here: 182 us
  Pallas kernels  85.9 us (47%)
  waiting for transfers between devices  36.6 us (20%)
  other arithmetic  19.7 us (11%)
  between operations  14.1 us (8%)
  local copies, waits for them, and re-layouts  14 us (8%)
  matrix products  10.2 us (6%)
    pallas_call x1, Pallas kernels, exchange(): pl.pallas_call(functools.partial(exchange_kernel, n_sect, n_dev), out_sha...  50 us
    reduce_scatter x1, waiting for transfers between devices, local(): lax.psum_scatter(partial_value, 'sect', scatter_dimension=1, tiled=True)  35.4 us
    pallas_call x1, Pallas kernels, products(): pl.pallas_call(functools.partial(product_kernel, own, vis_scale, beam_sca...  29.8 us
    dot_general x1, matrix products, local(): jnp.einsum('af,zfs->zas', matrix, voltages, preferred_element_type=jnp.fl...  10.2 us
    reshape x1, local copies, waits for them, and re-layouts, local(): jnp.transpose(gathered, (5, 2, 1, 3, 0, 4))  6.76 us
    concatenate x1, other arithmetic, beam_weights(): return jnp.concatenate([cosine, sine], axis=1)  6.55 us
    pallas_call x1, Pallas kernels, local(): pl.pallas_call(transform_kernel, out_shape=jax.ShapeDtypeStruct((n_dev, 2...  6.17 us
    convert_element_type x1, other arithmetic, beam_weights(): cosine = (ca * cb - sa * sb).astype(jnp.bfloat16).reshape(shape)  4.8 us
  transfers between devices with their start and end apart: 2, of which 2 were waited for; matrix products, arithmetic and copies ran while one was open for 10% of the time, Pallas kernels for 0%

profile of v1, /device:TPU:0, one launch (start us, length us, event | category | flops | bytes accessed | tf_op | source)
XLA Modules:
  0.0 182.2 jit_solution(13269895349773237554)
XLA Ops:
  7.2 0.0 reduce-scatter.2.cloned.1.call-start
  7.2 0.7 broadcast_compare_fusion
  7.9 10.2 %fusion = bf16[2,128,8192]{2,1,0:T(8,128)(2,1)} fusion(bf16[2,512,8192]{2,1,0:T(8,128)(2,1)} %param.5, s32[512]{0:T(512)} %param.7, pred[512]{0:T(512)(128)(4,1)S(1)} %broadcast_compare_fusion), kind=kOutput, calls=%fused_computation.4 | convolution fusion | flops 2149842944 | bytes 20974080 | tf_op jit(solution)/shard_map/af,zfs->zas/dot_general | solution.py:244
  18.1 0.0 reduce-scatter.2.cloned.1.call-update
  18.1 0.9 copy-done.2
  19.0 0.1 copy.10
  19.1 0.2 fusion.17
  19.2 0.4 fusion.15
  19.7 3.3 %add_convert_fusion.1 = (bf16[32,32,1024]{2,1,0:T(8,128)(2,1)}, bf16[32,32,1024]{2,1,0:T(8,128)(2,1)}) fusion(f32[32,1024]{1,0:T(8,128)S(1)} %get-tuple-element.24, f32[32,1024]{1,0:T(8,128)S(1)} %get-tuple-element.23, f32[32,1024]{1,0:T(8,128)S(1)} %fusion.17, f32[32,1024]{1,0:T(8,128)S(1)} %get-tuple-element.22), kind=kLoop, calls=%fused_computation.5 | loop fusion | flops 8388608 | bytes 4718592 | tf_op jit(solution)/shard_map/convert_element_type | solution.py:47
  23.0 1.3 fusion.7
  24.3 2.5 %fusion.1 = (f32[16,128,256]{2,1,0:T(8,128)S(1)}, f32[16,128,256]{2,1,0:T(8,128)S(1)}) fusion(f32[128,256]{1,0:T(8,128)S(1)} %copy.10), kind=kLoop, calls=%fused_computation.10 | loop fusion | flops 18874368 | bytes 4325376 | tf_op jit(solution)/shard_map/sub | solution.py:33
  26.8 4.8 %subtract_convert_fusion = (bf16[8,16,128,256]{3,2,1,0:T(8,128)(2,1)S(1)}, bf16[8,16,128,256]{3,2,1,0:T(8,128)(2,1)S(1)}) fusion(f32[16,128,256]{2,1,0:T(8,128)S(1)} %get-tuple-element.21, f32[8,128,256]{2,1,0:T(8,128)S(1)} %get-tuple-element.19, f32[16,128,256]{2,1,0:T(8,128)S(1)} %get-tuple-element.20, f32[8,128,256]{2,1,0:T(8,128)S(1)} %get-tuple-element.18), kind=kLoop, calls=%fused_computation.2 | loop fusion | flops 33554432 | bytes 23068672 | tf_op jit(solution)/shard_map/convert_element_type | solution.py:59
  31.6 6.5 %pad_maximum_fusion.weights = bf16[128,256,256]{2,1,0:T(8,128)(2,1)} fusion(bf16[128,128,256]{2,1,0:T(8,128)(2,1)S(1)} %bitcast.20, bf16[128,128,256]{2,1,0:T(8,128)(2,1)S(1)} %bitcast.19), kind=kLoop, calls=%fused_computation | loop fusion | flops 33554432 | bytes 33554432 | tf_op jit(solution)/shard_map/concatenate | solution.py:61
  38.1 35.4 %reduce-scatter.2.cloned.1.call-done.summed = bf16[2,32,8192]{2,1,0:T(8,128)(2,1)} async-done(((bf16[2,128,8192]{2,1,0:T(8,128)(2,1)}), bf16[2,32,8192]{2,1,0:T(8,128)(2,1)}) %reduce-scatter.2.cloned.1.call-update) | async-done | bytes 1048592 | tf_op jit(solution)/shard_map/reduce_scatter | solution.py:247
  73.6 1.0 slice.3
  74.6 1.8 collective-permute-start
  76.3 1.1 collective-permute-done.history
  77.5 0.8 copy-done.1
  78.2 6.2 %shard_map.68 = bf16[8,2,256,128]{3,2,1,0:T(8,128)(2,1)} custom-call(bf16[2,32,8192]{2,1,0:T(8,128)(2,1)} %reduce-scatter.2.cloned.1.call-done.summed, bf16[2,32,3072]{2,1,0:T(8,128)(2,1)} %copy-done.1, f32[4,1024]{1,0:T(4,128)} %taps.1, bf16[1024,1024]{1,0:T(8,128)(2,1)} %bitcast.23, bf16[1024,1024]{1,0:T(8,128)(2,1)} %bitcast.22), custom_call_target="tpu_custom_call" | custom-call | tf_op jit(solution)/shard_map/pallas_call | solution.py:257
  84.4 1.2 copy-done
  85.6 50.0 %shard_map.69 = bf16[4,8,512,128]{3,2,1,0:T(8,128)(2,1)S(1)} custom-call(bf16[8,512,128]{2,1,0:T(8,128)(2,1)S(1)} %bitcast.18), custom_call_target="tpu_custom_call" | custom-call | tf_op jit(solution)/shard_map/pallas_call | solution.py:170
  135.6 3.3 %copy.12 = bf16[4,8,2,8,32,128]{5,4,0,3,1,2:T(8,128)(2,1)} copy(bf16[4,8,2,8,32,128]{5,4,3,2,1,0:T(8,128)(2,1)S(1)} %bitcast.17) | data formatting | bytes 8388608 | tf_op jit(solution)/shard_map/reshape | solution.py:266
  138.9 6.8 %copy.13.volts = bf16[128,128,128]{2,1,0:T(8,128)(2,1)} copy(bf16[128,128,128]{0,2,1:T(8,128)(2,1)} %bitcast.21) | data formatting | bytes 8388608 | tf_op jit(solution)/shard_map/reshape | solution.py:267
  145.7 29.8 %shard_map.70 = (f32[2,128,32,128]{3,2,1,0:T(8,128)}, bf16[2,128,64,256]{3,2,1,0:T(8,128)(2,1)}) custom-call(bf16[128,128,128]{2,1,0:T(8,128)(2,1)} %copy.13.volts, bf16[128,256,256]{2,1,0:T(8,128)(2,1)} %pad_maximum_fusion.weights), custom_call_target="tpu_custom_call" | custom-call | tf_op jit(solution)/shard_map/pallas_call | solution.py:213
  (5 shorter events, 0.0 us)
Async XLA Ops:
  7.2 66.4 %reduce-scatter.2.cloned.1.call-start = ((), (), s32[]{:S(2)}) async-start(), calls=%async_computation.1 | async-start | bytes 5242880 | tf_op jit(solution)/shard_map/reduce_scatter | solution.py:247
  18.1 0.9 copy-start.2
  74.6 2.9 %collective-permute-start = (bf16[2,32,3072]{2,1,0:T(8,128)(2,1)S(1)}, bf16[2,32,3072]{2,1,0:T(8,128)(2,1)S(1)}, u32[]{:S(2)}, u32[]{:S(2)}) collective-permute-start(bf16[2,32,3072]{2,1,0:T(8,128)(2,1)S(1)} %slice.3), channel_id=1, source_target_pairs={{0,1},{1,2},{2,3},{3,4},{4,5},{5,6},{6,7},{8,9},{9,10},{10,11},{11... | collective-permute-start | bytes 1179656 | tf_op jit(solution)/shard_map/ppermute | solution.py:19
  77.5 0.8 copy-start.1
  84.4 1.2 copy-start
Sparse Core Ops, SparseCore 0:
  18.2 55.3 reduce-scatter.1

commit v2 on v1

--- a/solution.py
+++ b/solution.py
@@ -11,6 +11,8 @@
 FEEDS = 2048
 TILES = 128
 TAPS = 4
+LAG = 2
+BLOCK = 32
 
 
 def shifted(x, axis, by):
@@ -152,7 +154,7 @@
             copy.start()
             sends.append(copy)
 
-    lag = 1
+    lag = LAG
     for i in range(n_dev + lag):
         if i < n_dev:
             spread(order[i])
@@ -188,28 +190,27 @@
     count, both, _ = volts.shape
     half = both // 2
 
-    @pl.loop(0, count)
-    def _(c):
+    over_time = (((0,), (0,)), ((), ()))
+    for c in range(count):
         real, quad = volts[c, :half, :], volts[c, half:, :]
-        rows = jnp.concatenate(
-            [jnp.concatenate([real, quad], axis=1), jnp.concatenate([quad, -real], axis=1)], axis=0
-        )
+        straight = jnp.concatenate([real, quad], axis=1)
+        turned = jnp.concatenate([quad, -real], axis=1)
+        rows = jnp.concatenate([straight, turned], axis=0)
         beam = jnp.dot(rows, weights[c], preferred_element_type=jnp.float32) * beam_scale
         beams[0, c] = beam[:half].astype(jnp.bfloat16)
         beams[1, c] = beam[half:].astype(jnp.bfloat16)
-        right = jnp.concatenate([real, quad], axis=0)
-        turned = jnp.concatenate([quad, -real], axis=0)
-        over_time = (((0,), (0,)), ((), ()))
-        full[0] = lax.dot_general(right, right, over_time, preferred_element_type=jnp.float32)
-        full[1] = lax.dot_general(turned, right, over_time, preferred_element_type=jnp.float32)
-        vis[0, c] = full[0, pl.ds(first, own), :] * vis_scale
-        vis[1, c] = full[1, pl.ds(first, own), :] * vis_scale
+        right = volts[c]
+        left = jnp.concatenate([right, jnp.concatenate([quad, -real], axis=0)], axis=1)
+        full[c] = lax.dot_general(left, right, over_time, preferred_element_type=jnp.float32)
+        tiles = right.shape[1]
+        vis[0, c] = full[c, pl.ds(first, own), :] * vis_scale
+        vis[1, c] = full[c, pl.ds(pl.multiple_of(first + tiles, own), own), :] * vis_scale
 
 
 def products(volts, weights, own, vis_scale, beam_scale):
     chans, both, tiles = volts.shape
     beams = weights.shape[2]
-    block = 8
+    block = BLOCK
     return pl.pallas_call(
         functools.partial(product_kernel, own, vis_scale, beam_scale),
         grid=(chans // block,),
@@ -225,7 +226,7 @@
             pl.BlockSpec((2, block, own, tiles), lambda i: (0, i, 0, 0)),
             pl.BlockSpec((2, block, both // 2, beams), lambda i: (0, i, 0, 0)),
         ),
-        scratch_shapes=[pltpu.VMEM((2, tiles, tiles), jnp.float32)],
+        scratch_shapes=[pltpu.VMEM((block, 2 * tiles, tiles), jnp.float32)],
     )(volts, weights)
 
 

time: 183 us -> 164 us (0.90)
  Pallas kernels: 85.9 us -> 67.5 us
    pallas_call x1, Pallas kernels: 29.8 us -> 13.2 us  [products(): pl.pallas_call(functools.partial(product_kernel, own, vis_scale, beam_sca...]
    pallas_call x1, Pallas kernels: 50 us -> 48.1 us  [exchange(): pl.pallas_call(functools.partial(exchange_kernel, n_sect, n_dev), out_sha...]
  transfers between devices with their start and end apart: 2 -> 2, of which waited for: 2 -> 2; matrix products, arithmetic and copies ran while one was open for 10% -> 12% of each run, Pallas kernels for 0% -> 0%
where the time goes in v2:
time: 164 us
  Pallas kernels  67.5 us (41%)
  waiting for transfers between devices  36.6 us (22%)
  other arithmetic  19.7 us (12%)
  between operations  14.1 us (9%)
  local copies, waits for them, and re-layouts  14 us (9%)
  matrix products  10.2 us (6%)
  starting transfers between devices  1.8 us (1%)
    pallas_call x1, Pallas kernels, exchange(): pl.pallas_call(functools.partial(exchange_kernel, n_sect, n_dev), out_sha...  48.1 us
    reduce_scatter x1, waiting for transfers between devices, local(): lax.psum_scatter(partial_value, 'sect', scatter_dimension=1, tiled=True)  35.4 us
    pallas_call x1, Pallas kernels, products(): pl.pallas_call(functools.partial(product_kernel, own, vis_scale, beam_sca...  13.2 us
    dot_general x1, matrix products, local(): jnp.einsum('af,zfs->zas', matrix, voltages, preferred_element_type=jnp.fl...  10.2 us
    reshape x1, local copies, waits for them, and re-layouts, local(): jnp.transpose(gathered, (5, 2, 1, 3, 0, 4))  6.76 us
    concatenate x1, other arithmetic, beam_weights(): return jnp.concatenate([cosine, sine], axis=1)  6.55 us
    pallas_call x1, Pallas kernels, local(): pl.pallas_call(transform_kernel, out_shape=jax.ShapeDtypeStruct((n_dev, 2...  6.17 us
    convert_element_type x1, other arithmetic, beam_weights(): cosine = (ca * cb - sa * sb).astype(jnp.bfloat16).reshape(shape)  4.8 us
  transfers between devices with their start and end apart: 2, of which 2 were waited for; matrix products, arithmetic and copies ran while one was open for 12% of the time, Pallas kernels for 0%

profile of v2, /device:TPU:0, one launch (start us, length us, event | category | flops | bytes accessed | tf_op | source)
XLA Modules:
  0.0 163.8 jit_solution(17875904227919288251)
XLA Ops:
  7.2 0.0 reduce-scatter.2.cloned.1.call-start
  7.2 0.7 broadcast_compare_fusion
  7.9 10.2 %fusion = bf16[2,128,8192]{2,1,0:T(8,128)(2,1)} fusion(bf16[2,512,8192]{2,1,0:T(8,128)(2,1)} %param.5, s32[512]{0:T(512)} %param.7, pred[512]{0:T(512)(128)(4,1)S(1)} %broadcast_compare_fusion), kind=kOutput, calls=%fused_computation.4 | convolution fusion | flops 2149842944 | bytes 20974080 | tf_op jit(solution)/shard_map/af,zfs->zas/dot_general | solution.py:245
  18.1 0.0 reduce-scatter.2.cloned.1.call-update
  18.1 0.9 copy-done.2
  19.0 0.1 copy.10
  19.1 0.2 fusion.17
  19.2 0.4 fusion.15
  19.7 3.3 %add_convert_fusion.1 = (bf16[32,32,1024]{2,1,0:T(8,128)(2,1)}, bf16[32,32,1024]{2,1,0:T(8,128)(2,1)}) fusion(f32[32,1024]{1,0:T(8,128)S(1)} %get-tuple-element.24, f32[32,1024]{1,0:T(8,128)S(1)} %get-tuple-element.23, f32[32,1024]{1,0:T(8,128)S(1)} %fusion.17, f32[32,1024]{1,0:T(8,128)S(1)} %get-tuple-element.22), kind=kLoop, calls=%fused_computation.5 | loop fusion | flops 8388608 | bytes 4718592 | tf_op jit(solution)/shard_map/convert_element_type | solution.py:49
  23.0 1.3 fusion.7
  24.3 2.5 %fusion.1 = (f32[16,128,256]{2,1,0:T(8,128)S(1)}, f32[16,128,256]{2,1,0:T(8,128)S(1)}) fusion(f32[128,256]{1,0:T(8,128)S(1)} %copy.10), kind=kLoop, calls=%fused_computation.10 | loop fusion | flops 18874368 | bytes 4325376 | tf_op jit(solution)/shard_map/sub | solution.py:35
  26.8 4.8 %subtract_convert_fusion = (bf16[8,16,128,256]{3,2,1,0:T(8,128)(2,1)S(1)}, bf16[8,16,128,256]{3,2,1,0:T(8,128)(2,1)S(1)}) fusion(f32[16,128,256]{2,1,0:T(8,128)S(1)} %get-tuple-element.21, f32[8,128,256]{2,1,0:T(8,128)S(1)} %get-tuple-element.19, f32[16,128,256]{2,1,0:T(8,128)S(1)} %get-tuple-element.20, f32[8,128,256]{2,1,0:T(8,128)S(1)} %get-tuple-element.18), kind=kLoop, calls=%fused_computation.2 | loop fusion | flops 33554432 | bytes 23068672 | tf_op jit(solution)/shard_map/convert_element_type | solution.py:61
  31.6 6.5 %pad_maximum_fusion.weights = bf16[128,256,256]{2,1,0:T(8,128)(2,1)} fusion(bf16[128,128,256]{2,1,0:T(8,128)(2,1)S(1)} %bitcast.20, bf16[128,128,256]{2,1,0:T(8,128)(2,1)S(1)} %bitcast.19), kind=kLoop, calls=%fused_computation | loop fusion | flops 33554432 | bytes 33554432 | tf_op jit(solution)/shard_map/concatenate | solution.py:63
  38.1 35.4 %reduce-scatter.2.cloned.1.call-done.summed = bf16[2,32,8192]{2,1,0:T(8,128)(2,1)} async-done(((bf16[2,128,8192]{2,1,0:T(8,128)(2,1)}), bf16[2,32,8192]{2,1,0:T(8,128)(2,1)}) %reduce-scatter.2.cloned.1.call-update) | async-done | bytes 1048592 | tf_op jit(solution)/shard_map/reduce_scatter | solution.py:248
  73.6 1.0 slice.3
  74.6 1.8 %collective-permute-start = (bf16[2,32,3072]{2,1,0:T(8,128)(2,1)S(1)}, bf16[2,32,3072]{2,1,0:T(8,128)(2,1)S(1)}, u32[]{:S(2)}, u32[]{:S(2)}) collective-permute-start(bf16[2,32,3072]{2,1,0:T(8,128)(2,1)S(1)} %slice.3), channel_id=1, source_target_pairs={{0,1},{1,2},{2,3},{3,4},{4,5},{5,6},{6,7},{8,9},{9,10},{10,11},{11... | collective-permute-start | bytes 1179656 | tf_op jit(solution)/shard_map/ppermute | solution.py:21
  76.3 1.1 collective-permute-done.history
  77.5 0.8 copy-done.1
  78.2 6.2 %shard_map.68 = bf16[8,2,256,128]{3,2,1,0:T(8,128)(2,1)} custom-call(bf16[2,32,8192]{2,1,0:T(8,128)(2,1)} %reduce-scatter.2.cloned.1.call-done.summed, bf16[2,32,3072]{2,1,0:T(8,128)(2,1)} %copy-done.1, f32[4,1024]{1,0:T(4,128)} %taps.1, bf16[1024,1024]{1,0:T(8,128)(2,1)} %bitcast.23, bf16[1024,1024]{1,0:T(8,128)(2,1)} %bitcast.22), custom_call_target="tpu_custom_call" | custom-call | tf_op jit(solution)/shard_map/pallas_call | solution.py:258
  84.4 1.2 copy-done
  85.6 48.1 %shard_map.69 = bf16[4,8,512,128]{3,2,1,0:T(8,128)(2,1)S(1)} custom-call(bf16[8,512,128]{2,1,0:T(8,128)(2,1)S(1)} %bitcast.18), custom_call_target="tpu_custom_call" | custom-call | tf_op jit(solution)/shard_map/pallas_call | solution.py:172
  133.7 3.3 %copy.12 = bf16[4,8,2,8,32,128]{5,4,0,3,1,2:T(8,128)(2,1)} copy(bf16[4,8,2,8,32,128]{5,4,3,2,1,0:T(8,128)(2,1)S(1)} %bitcast.17) | data formatting | bytes 8388608 | tf_op jit(solution)/shard_map/reshape | solution.py:267
  137.0 6.8 %copy.13.volts = bf16[128,128,128]{2,1,0:T(8,128)(2,1)} copy(bf16[128,128,128]{0,2,1:T(8,128)(2,1)} %bitcast.21) | data formatting | bytes 8388608 | tf_op jit(solution)/shard_map/reshape | solution.py:268
  143.8 13.2 %shard_map.70 = (f32[2,128,32,128]{3,2,1,0:T(8,128)}, bf16[2,128,64,256]{3,2,1,0:T(8,128)(2,1)}) custom-call(bf16[128,128,128]{2,1,0:T(8,128)(2,1)} %copy.13.volts, bf16[128,256,256]{2,1,0:T(8,128)(2,1)} %pad_maximum_fusion.weights), custom_call_target="tpu_custom_call" | custom-call | tf_op jit(solution)/shard_map/pallas_call | solution.py:214
  (5 shorter events, 0.0 us)
Async XLA Ops:
  7.2 66.4 %reduce-scatter.2.cloned.1.call-start = ((), (), s32[]{:S(2)}) async-start(), calls=%async_computation.1 | async-start | bytes 5242880 | tf_op jit(solution)/shard_map/reduce_scatter | solution.py:248
  18.1 0.9 copy-start.2
  74.6 2.9 %collective-permute-start = (bf16[2,32,3072]{2,1,0:T(8,128)(2,1)S(1)}, bf16[2,32,3072]{2,1,0:T(8,128)(2,1)S(1)}, u32[]{:S(2)}, u32[]{:S(2)}) collective-permute-start(bf16[2,32,3072]{2,1,0:T(8,128)(2,1)S(1)} %slice.3), channel_id=1, source_target_pairs={{0,1},{1,2},{2,3},{3,4},{4,5},{5,6},{6,7},{8,9},{9,10},{10,11},{11... | collective-permute-start | bytes 1179656 | tf_op jit(solution)/shard_map/ppermute | solution.py:21
  77.5 0.8 copy-start.1
  84.4 1.2 copy-start
Sparse Core Ops, SparseCore 0:
  18.2 55.3 reduce-scatter.1

commit v3 on v2

--- a/solution.py
+++ b/solution.py
@@ -66,20 +66,94 @@
 VMEM = pl.BlockSpec(memory_space=pltpu.VMEM)
 
 
+def scatter_kernel(n_sect, matrix, volts, out, part, land, b_send, b_recv):
+    me_s, me_d = lax.axis_index("sect"), lax.axis_index("dev")
+    i, steps = pl.program_id(0), pl.num_programs(0)
+    own = matrix.shape[0] // n_sect
+    width = volts.shape[2]
+    mesh_id = pl.DeviceIdType.MESH
+
+    @pl.when(i == 0)
+    def _():
+        barrier = pltpu.get_barrier_semaphore()
+        for j in range(1, n_sect):
+            pl.semaphore_signal(
+                barrier, inc=1, device_id=(lax.rem(me_s + j, n_sect), me_d), device_id_type=mesh_id
+            )
+        pl.semaphore_wait(barrier, n_sect - 1)
+
+    def push(block, j):
+        dest = lax.rem(me_s + j, n_sect)
+        return pltpu.make_async_remote_copy(
+            src_ref=part.at[block, dest], dst_ref=land.at[block, j],
+            send_sem=b_send.at[block, j], recv_sem=b_recv.at[block, j],
+            device_id=(dest, me_d), device_id_type=mesh_id,
+        )
+
+    total = jnp.dot(matrix[...], volts[0], preferred_element_type=jnp.float32)
+    total = total.astype(jnp.bfloat16)
+    for s in range(n_sect):
+        part[i, s] = total[s * own : (s + 1) * own]
+
+    @pl.when(i > 0)
+    def _():
+        for j in range(1, n_sect):
+            push(i - 1, j).start()
+
+    @pl.when(i == steps - 1)
+    def _():
+        for j in range(1, n_sect):
+            push(i, j).start()
+
+        @pl.loop(0, part.shape[0])
+        def _(block):
+            running = part[block, me_s].astype(jnp.float32)
+            for j in range(1, n_sect):
+                push(block, j).wait_recv()
+                running = running + land[block, j].astype(jnp.float32)
+            out[block] = running.astype(jnp.bfloat16)
+
+        @pl.loop(0, part.shape[0])
+        def _(block):
+            for j in range(1, n_sect):
+                push(block, j).wait_send()
+
+
+def scatter(matrix, voltages, n_sect, width):
+    _, feeds, samples = voltages.shape
+    across = samples // width
+    steps = 2 * across
+    own = matrix.shape[0] // n_sect
+    dma = pltpu.SemaphoreType.DMA
+    return pl.pallas_call(
+        functools.partial(scatter_kernel, n_sect),
+        grid=(steps,),
+        out_shape=jax.ShapeDtypeStruct((steps, own, width), jnp.bfloat16),
+        in_specs=[
+            pl.BlockSpec(matrix.shape, lambda i: (0, 0)),
+            pl.BlockSpec((1, feeds, width), lambda i: (i // across, 0, lax.rem(i, across))),
+        ],
+        out_specs=VMEM,
+        scratch_shapes=[
+            pltpu.VMEM((steps, n_sect, own, width), jnp.bfloat16),
+            pltpu.VMEM((steps, n_sect, own, width), jnp.bfloat16),
+            dma((steps, n_sect)), dma((steps, n_sect)),
+        ],
+        compiler_params=pltpu.CompilerParams(
+            collective_id=1, has_side_effects=True, vmem_limit_bytes=60 * 2**20
+        ),
+    )(matrix, voltages)
+
+
 def transform_kernel(summed, history, taps, cosine, sine, out, filtered):
     n_dest, _, _, width = out.shape
-    own = summed.shape[1]
+    frames, own = summed.shape[1:3]
     channels = taps.shape[1]
-    frames = summed.shape[2] // channels
     for z in range(2):
         for t in range(frames):
             total = 0.0
             for m in range(TAPS):
-                if t >= m:
-                    block = summed[z, :, (t - m) * channels : (t - m + 1) * channels]
-                else:
-                    at = t - m + TAPS - 1
-                    block = history[z, :, at * channels : (at + 1) * channels]
+                block = summed[z, t - m] if t >= m else history[z, t - m + TAPS - 1]
                 total = total + taps[m : m + 1, :] * block.astype(jnp.float32)
             filtered[z, t * own : (t + 1) * own, :] = total.astype(jnp.bfloat16)
     step = max(256, width)
@@ -233,7 +307,6 @@
 def local(voltages, filter_taps, feed_tile, bad_feed, delays):
     channels = filter_taps.shape[1]
     local_frames = voltages.shape[2] // channels
-    rim = (TAPS - 1) * channels
     n_dev = lax.axis_size("dev")
     n_sect = lax.axis_size("sect")
     local_chans = channels // n_dev
@@ -242,19 +315,14 @@
     tile_ids = jnp.arange(TILES, dtype=jnp.int32)
     member = (feed_tile[None, :] == tile_ids[:, None]) & (bad_feed[None, :] == 0)
     matrix = jnp.where(member, 1.0, 0.0).astype(jnp.bfloat16)
-    partial_value = jnp.einsum(
-        "af,zfs->zas", matrix, voltages, preferred_element_type=jnp.float32
-    ).astype(jnp.bfloat16)
-    summed = lax.psum_scatter(partial_value, "sect", scatter_dimension=1, tiled=True)
-    own = summed.shape[1]
-
     cosine, sine = fourier_tables(channels)
     weights = beam_weights(
         delays, lax.axis_index("dev") * local_chans, local_chans, channels
     )
-    summed, cosine, sine, weights = lax.optimization_barrier((summed, cosine, sine, weights))
-
-    history = shifted(summed[:, :, summed.shape[2] - rim :], "dev", 1)
+    own = TILES // n_sect
+    summed = scatter(matrix, voltages, n_sect, channels).reshape(2, local_frames, own, channels)
+
+    history = shifted(summed[:, local_frames - (TAPS - 1) :], "dev", 1)
     blocks = pl.pallas_call(
         transform_kernel,
         out_shape=jax.ShapeDtypeStruct((n_dev, 2, local_frames * own, local_chans), jnp.bfloat16),

time: 164 us -> 157 us (0.957)
  Pallas kernels: 67.5 us -> 118 us
  waiting for transfers between devices: 36.6 us -> 0.01 us
  between operations: 14.1 us -> 0.72 us
  matrix products: 10.2 us -> 0 us
  other arithmetic: 19.7 us -> 22.1 us
    pallas_call x0 -> x1, Pallas kernels: none -> 54.1 us  [scatter(): pl.pallas_call(functools.partial(scatter_kernel, n_sect), grid=(steps,),...]
    reduce_scatter x1 -> x0, waiting for transfers between devices: 35.4 us -> none  [local(): lax.psum_scatter(partial_value, 'sect', scatter_dimension=1, tiled=True)]
    dot_general x1 -> x0, matrix products: 10.2 us -> none  [local(): jnp.einsum('af,zfs->zas', matrix, voltages, preferred_element_type=jnp.fl...]
    pallas_call x1, Pallas kernels: 48.1 us -> 44.9 us  [exchange(): pl.pallas_call(functools.partial(exchange_kernel, n_sect, n_dev), out_sha...]
  transfers between devices with their start and end apart: 2 -> 1, of which waited for: 2 -> 0; matrix products, arithmetic and copies ran while one was open for 12% -> 13% of each run, Pallas kernels for 0% -> 0%
where the time goes in v3:
time: 157 us; the launch traced here: 156 us
  Pallas kernels  118 us (75%)
  other arithmetic  22.1 us (14%)
  local copies, waits for them, and re-layouts  13.2 us (8%)
  starting transfers between devices  1.57 us (1%)
    pallas_call x1, Pallas kernels, scatter(): pl.pallas_call(functools.partial(scatter_kernel, n_sect), grid=(steps,),...  54.1 us
    pallas_call x1, Pallas kernels, exchange(): pl.pallas_call(functools.partial(exchange_kernel, n_sect, n_dev), out_sha...  44.9 us
    pallas_call x1, Pallas kernels, products(): pl.pallas_call(functools.partial(product_kernel, own, vis_scale, beam_sca...  13.2 us
    reshape x1, local copies, waits for them, and re-layouts, local(): jnp.transpose(gathered, (5, 2, 1, 3, 0, 4))  6.76 us
    concatenate x1, other arithmetic, beam_weights(): return jnp.concatenate([cosine, sine], axis=1)  6.54 us
    pallas_call x1, Pallas kernels, local(): pl.pallas_call(transform_kernel, out_shape=jax.ShapeDtypeStruct((n_dev, 2...  6.21 us
    sub x3, other arithmetic, turn_trig(): return (1.0 - 2.0 * s * s, 2.0 * s * c)  4.93 us
    convert_element_type x1, other arithmetic, beam_weights(): cosine = (ca * cb - sa * sb).astype(jnp.bfloat16).reshape(shape)  4.8 us
  transfers between devices with their start and end apart: 1, of which 0 were waited for; matrix products, arithmetic and copies ran while one was open for 13% of the time, Pallas kernels for 0%

profile of v3, /device:TPU:0, one launch (start us, length us, event | category | flops | bytes accessed | tf_op | source)
XLA Modules:
  0.0 155.9 jit_solution(6265066837240016173)
XLA Ops:
  0.6 0.7 broadcast_compare_fusion
  1.3 1.4 select_convert_fusion.matrix
  2.7 0.0 copy-start.3
  2.7 54.1 %shard_map.68 = bf16[16,32,1024]{2,1,0:T(8,128)(2,1)} custom-call(bf16[128,512]{1,0:T(8,128)(2,1)} %select_convert_fusion.matrix, bf16[2,512,8192]{2,1,0:T(8,128)(2,1)} %volts.1), custom_call_target="tpu_custom_call" | custom-call | tf_op jit(solution)/shard_map/pallas_call | solution.py:128
  56.8 1.0 slice.4
  57.8 1.6 %collective-permute-start = (bf16[2,3,32,1024]{3,2,1,0:T(8,128)(2,1)S(1)}, bf16[2,3,32,1024]{3,2,1,0:T(8,128)(2,1)S(1)}, u32[]{:S(2)}, u32[]{:S(2)}) collective-permute-start(bf16[2,3,32,1024]{3,2,1,0:T(8,128)(2,1)S(1)} %slice.4), channel_id=1, source_target_pairs={{0,1},{1,2},{2,3},{3,4},{4,5},{5,6},{6,7},{8,9},{9,10},{10,11},{11... | collective-permute-start | bytes 1179656 | tf_op jit(solution)/shard_map/ppermute | solution.py:21
  59.4 0.0 copy-done.3
  59.4 0.1 copy.11
  59.5 3.5 %fusion = (f32[16,128,256]{2,1,0:T(8,128)S(1)}, f32[16,128,256]{2,1,0:T(8,128)}) fusion(f32[128,256]{1,0:T(8,128)S(1)} %copy.11), kind=kLoop, calls=%fused_computation.8 | loop fusion | flops 18874368 | bytes 4325376 | tf_op jit(solution)/shard_map/sub | solution.py:35
  63.0 1.3 fusion.6
  64.3 0.4 fusion.14
  64.7 0.0 copy-done.1
  64.8 4.8 %subtract_convert_fusion = (bf16[8,16,128,256]{3,2,1,0:T(8,128)(2,1)S(1)}, bf16[8,16,128,256]{3,2,1,0:T(8,128)(2,1)S(1)}) fusion(f32[16,128,256]{2,1,0:T(8,128)S(1)} %copy-done.1, f32[8,128,256]{2,1,0:T(8,128)S(1)} %get-tuple-element.11, f32[16,128,256]{2,1,0:T(8,128)S(1)} %get-tuple-element.12, f32[8,128,256]{2,1,0:T(8,128)S(1)} %get-tuple-element.10), kind=kLoop, calls=%fused_computation.2 | loop fusion | flops 33554432 | bytes 23068672 | tf_op jit(solution)/shard_map/convert_element_type | solution.py:61
  69.6 6.5 %pad_maximum_fusion.weights = bf16[128,256,256]{2,1,0:T(8,128)(2,1)} fusion(bf16[128,128,256]{2,1,0:T(8,128)(2,1)S(1)} %bitcast.15, bf16[128,128,256]{2,1,0:T(8,128)(2,1)S(1)} %bitcast.14), kind=kLoop, calls=%fused_computation | loop fusion | flops 33554432 | bytes 33554432 | tf_op jit(solution)/shard_map/concatenate | solution.py:63
  76.1 0.2 fusion.16
  76.3 3.3 %add_convert_fusion.1 = (bf16[32,32,1024]{2,1,0:T(8,128)(2,1)}, bf16[32,32,1024]{2,1,0:T(8,128)(2,1)}) fusion(f32[32,1024]{1,0:T(8,128)S(1)} %get-tuple-element.16, f32[32,1024]{1,0:T(8,128)S(1)} %get-tuple-element.15, f32[32,1024]{1,0:T(8,128)S(1)} %fusion.16, f32[32,1024]{1,0:T(8,128)S(1)} %get-tuple-element.14), kind=kLoop, calls=%fused_computation.3 | loop fusion | flops 8388608 | bytes 4718592 | tf_op jit(solution)/shard_map/convert_element_type | solution.py:49
  79.6 0.0 collective-permute-done.history
  79.6 0.7 copy-done.2
  80.3 6.2 %shard_map.69 = bf16[8,2,256,128]{3,2,1,0:T(8,128)(2,1)} custom-call(bf16[2,8,32,1024]{3,2,1,0:T(8,128)(2,1)} %bitcast.20, bf16[2,3,32,1024]{3,2,1,0:T(8,128)(2,1)} %copy-done.2, f32[4,1024]{1,0:T(4,128)} %taps.1, bf16[1024,1024]{1,0:T(8,128)(2,1)} %bitcast.18, bf16[1024,1024]{1,0:T(8,128)(2,1)} %bitcast.17), custom_call_target="tpu_custom_call" | custom-call | tf_op jit(solution)/shard_map/pallas_call | solution.py:326
  86.5 1.2 copy-done
  87.8 44.9 %shard_map.70 = bf16[4,8,512,128]{3,2,1,0:T(8,128)(2,1)S(1)} custom-call(bf16[8,512,128]{2,1,0:T(8,128)(2,1)S(1)} %bitcast.13), custom_call_target="tpu_custom_call" | custom-call | tf_op jit(solution)/shard_map/pallas_call | solution.py:246
  132.7 3.3 %copy.10 = bf16[4,8,2,8,32,128]{5,4,0,3,1,2:T(8,128)(2,1)} copy(bf16[4,8,2,8,32,128]{5,4,3,2,1,0:T(8,128)(2,1)S(1)} %bitcast.12) | data formatting | bytes 8388608 | tf_op jit(solution)/shard_map/reshape | solution.py:335
  136.0 6.8 %copy.13.volts = bf16[128,128,128]{2,1,0:T(8,128)(2,1)} copy(bf16[128,128,128]{0,2,1:T(8,128)(2,1)} %bitcast.16) | data formatting | bytes 8388608 | tf_op jit(solution)/shard_map/reshape | solution.py:336
  142.7 13.2 %shard_map.71 = (f32[2,128,32,128]{3,2,1,0:T(8,128)}, bf16[2,128,64,256]{3,2,1,0:T(8,128)(2,1)}) custom-call(bf16[128,128,128]{2,1,0:T(8,128)(2,1)} %copy.13.volts, bf16[128,256,256]{2,1,0:T(8,128)(2,1)} %pad_maximum_fusion.weights), custom_call_target="tpu_custom_call" | custom-call | tf_op jit(solution)/shard_map/pallas_call | solution.py:288
  (5 shorter events, 0.0 us)
Async XLA Ops:
  2.7 56.7 %copy-start.3 = (f32[256,128]{1,0:T(8,128)S(1)}, f32[256,128]{1,0:T(8,128)}, u32[]{:S(2)}) copy-start(f32[256,128]{1,0:T(8,128)} %param.9) | copy-start | bytes 393220
  57.8 21.7 %collective-permute-start = (bf16[2,3,32,1024]{3,2,1,0:T(8,128)(2,1)S(1)}, bf16[2,3,32,1024]{3,2,1,0:T(8,128)(2,1)S(1)}, u32[]{:S(2)}, u32[]{:S(2)}) collective-permute-start(bf16[2,3,32,1024]{3,2,1,0:T(8,128)(2,1)S(1)} %slice.4), channel_id=1, source_target_pairs={{0,1},{1,2},{2,3},{3,4},{4,5},{5,6},{6,7},{8,9},{9,10},{10,11},{11... | collective-permute-start | bytes 1179656 | tf_op jit(solution)/shard_map/ppermute | solution.py:21
  63.0 1.8 %copy-start.1 = (f32[16,128,256]{2,1,0:T(8,128)S(1)}, f32[16,128,256]{2,1,0:T(8,128)}, u32[]{:S(2)}) copy-start(f32[16,128,256]{2,1,0:T(8,128)} %get-tuple-element.13) | copy-start | bytes 6291460
  79.6 0.7 copy-start.2
  86.5 1.2 copy-start
